TPU v7x, 32 devices: a whole 2x2x4 slice. The times are simulated.
32 devices in a mesh: dp: 4 (over y, x), feat: 8 (over z, core).
Axes of the slice: x: 2, y: 2, z: 4, core: 2. Of those that a mesh axis runs over, the one named last changes fastest.
Arguments:
- features: bfloat16 [8192, 1024], P('dp', 'feat'), may hold values from -6 to 6
- owners: int32 [8, 64, 1], P('feat', 'dp'), may hold values from 0 to 3; in each aligned block of 16 rows (0 to 15, 16 to 31, ..., all dimensions but the last counted through in order) at most 8 rows name the same one
- weights: bfloat16 [8, 4096], P(None, ('dp', 'feat')), may hold values from -0.1875 to 0.1875
- labels: int32 [8192], P('dp'), may hold values from 0 to 7
Outputs:
- hessian: float32 [32, 1024, 1024], P(('dp', 'feat'))
- gradient: float32 [8, 4096], P(None, ('dp', 'feat'))
Inputs may be any that keep to these rules, and one draw needn't show every extreme that they name: `owners`: among the 16 row blocks of one index of dp, in one tile column, at most 8 name the same owner, a bound that some block reaches.
All inputs are finite; a program needn't handle non-finite values.
Results may differ from a plain program's by a relative error of at most 0.0023.
Values may be sent and summed in bfloat16 or wider, within the bound.
A program may use at most 64 MiB of HBM per device.

v0:
```python
import math
import jax
import jax.numpy as jnp
from jax import lax
from jax.sharding import PartitionSpec as P


def normalize(logits):
    expo = jnp.exp(logits)
    return expo / jnp.sum(expo, axis=-1, keepdims=True)


def spread_diagonal(diag_part, classes, width):
    blocks = diag_part.reshape(classes, width, width)
    unit = jnp.eye(classes, dtype=jnp.float32)
    return (unit[:, None, :, None] * blocks[:, :, None, :]).reshape(
        classes * width, classes * width
    )


def arrange(target, groups, capacity):
    count = target.shape[0]
    order = jnp.arange(count, dtype=jnp.int32)
    earlier = (order[None, :] < order[:, None]) & (target[None, :] == target[:, None])
    ranking = jnp.sum(earlier.astype(jnp.int32), axis=1)
    slot_index = jnp.arange(groups * capacity, dtype=jnp.int32)
    slot_group = slot_index // capacity
    slot_rank = slot_index % capacity
    hits = (target[None, :] == slot_group[:, None]) & (ranking[None, :] == slot_rank[:, None])
    source = jnp.sum(jnp.where(hits, order[None, :], 0), axis=1)
    filled = jnp.any(hits, axis=1)
    return (source, filled)


def select_blocks(block_data, source, filled):
    picked = jnp.take(block_data, source, axis=0)
    return jnp.where(filled[:, None, None], picked, jnp.zeros_like(picked))


def accumulate(totals, feature_rows, prob_rows, classes):
    count, width = feature_rows.shape
    group = math.gcd(count, 512)

    def turn(step, state):
        hess_acc, grad_acc = state
        begin = step * group
        x_part = lax.dynamic_slice_in_dim(feature_rows, begin, group, 0)
        p_part = lax.dynamic_slice_in_dim(prob_rows, begin, group, 0)
        probs = p_part[:, :classes].astype(jnp.float32)
        resid = p_part[:, classes:]
        kron_rows = (
            (probs[:, :, None] * x_part.astype(jnp.float32)[:, None, :])
            .reshape(group, classes * width)
            .astype(jnp.bfloat16)
        )
        joint = jnp.concatenate([kron_rows, x_part], axis=1)
        product = lax.dot_general(
            kron_rows, joint, (((0,), (0,)), ((), ())), preferred_element_type=jnp.float32
        )
        square = product[:, : classes * width]
        diag_part = product[:, classes * width :]
        grad_term = lax.dot_general(
            resid, x_part, (((0,), (0,)), ((), ())), preferred_element_type=jnp.float32
        )
        return (
            hess_acc + spread_diagonal(diag_part, classes, width) - square,
            grad_acc + grad_term,
        )

    return lax.fori_loop(0, count // group, turn, totals)


def per_device(features, owners, weights, labels):
    rows, width = features.shape
    classes = weights.shape[0]
    blocks = owners.shape[1]
    block_rows = rows // blocks
    dp_count = lax.axis_size("dp")
    capacity = max(2, 2 * ((blocks + dp_count - 1) // dp_count))
    target = owners.reshape(blocks)
    gathered = lax.all_gather(weights, "dp", axis=1, tiled=True)
    table = gathered.reshape(classes, dp_count, width)
    every_owner = jnp.einsum("rt,cut->ruc", features, table, preferred_element_type=jnp.float32)
    row_owner = jnp.repeat(target, block_rows)
    owner_mask = (row_owner[:, None] == jnp.arange(dp_count, dtype=jnp.int32)[None, :]).astype(
        jnp.float32
    )
    partial_logits = jnp.sum(every_owner * owner_mask[:, :, None], axis=1)
    logits = lax.psum(partial_logits, "feat")
    probs = normalize(logits)
    onehot = (labels[:, None] == jnp.arange(classes, dtype=jnp.int32)[None, :]).astype(jnp.float32)
    probs_half = probs.astype(jnp.bfloat16)
    resid = (probs - onehot).astype(jnp.bfloat16)
    paired = jnp.concatenate([probs_half, resid], axis=1)
    feature_blocks = features.reshape(blocks, block_rows, width)
    paired_blocks = paired.reshape(blocks, block_rows, 2 * classes)
    start = (
        jnp.zeros((classes * width, classes * width), jnp.float32),
        jnp.zeros((classes, width), jnp.float32),
    )
    source, filled = arrange(target, dp_count, capacity)
    sent_features = select_blocks(feature_blocks, source, filled)
    sent_paired = select_blocks(paired_blocks, source, filled)
    got_features, got_paired = (
        lax.all_to_all(sent_features, "dp", split_axis=0, concat_axis=0, tiled=True),
        lax.all_to_all(sent_paired, "dp", split_axis=0, concat_axis=0, tiled=True),
    )
    hess_acc, grad_acc = accumulate(
        start, got_features.reshape(-1, width), got_paired.reshape(-1, 2 * classes), classes
    )
    hessian = (hess_acc / block_rows)[None]
    gradient = grad_acc / block_rows
    return (hessian, gradient)


def solution(mesh):
    in_specs = (P("dp", "feat"), P("feat", "dp", None), P(None, ("dp", "feat")), P("dp"))
    out_specs = (P(("dp", "feat"), None, None), P(None, ("dp", "feat")))
    return jax.shard_map(
        per_device, mesh=mesh, in_specs=in_specs, out_specs=out_specs, check_vma=False
    )
```

profile of v0, /device:TPU:0, one launch (start us, length us, event | category | flops | bytes accessed | tf_op | source)
XLA Modules:
  0.0 189.6 jit_solution(15932147110795025760)
XLA Ops:
  7.2 0.8 broadcast_bitcast_fusion
  8.0 9.6 %all_gather.3 = bf16[8,512]{1,0:T(8,128)(2,1)S(1)} all-gather(bf16[8,128]{1,0:T(8,128)(2,1)} %param.8), channel_id=1, replica_groups=mesh['dp'=4,'feat'=8] {'dp'}, dimensions={1}, use_global_device_ids=true | all-gather | bytes 10240 | tf_op jit(solution)/shard_map/all_gather | solution.py:81
  17.7 0.9 fusion.9
  18.6 0.9 convert_reduce_fusion
  21.0 0.7 gather_fusion.1
  21.8 50.8 %all-reduce.2.cloned.1.call-done = f32[2048,8]{0,1:T(8,128)} async-done(((f32[2048,8]{0,1:T(8,128)}), f32[2048,8]{0,1:T(8,128)}) %all-reduce.2.cloned.1.call-update) | async-done | bytes 65552 | tf_op jit(solution)/shard_map/psum | solution.py:89
  72.6 0.9 exponential_reduce_fusion
  73.5 0.9 fusion.12
  75.0 0.8 select_select_fusion.1
  75.8 3.6 %all-to-all-start = ((bf16[32,128,16]{1,2,0:T(8,128)(2,1)}), bf16[32,128,16]{1,2,0:T(8,128)(2,1)S(1)}, u32[]{:S(2)}, u32[]{:S(2)}) async-start(bf16[32,128,16]{1,2,0:T(8,128)(2,1)} %select_select_fusion.1), calls=%async_computation | async-start | bytes 262144 | tf_op jit(solution)/shard_map/all_to_all | solution.py:106
  79.4 1.2 select_select_fusion
  80.6 3.8 %all-to-all-done = bf16[32,128,16]{1,2,0:T(8,128)(2,1)S(1)} async-done(((bf16[32,128,16]{1,2,0:T(8,128)(2,1)}), bf16[32,128,16]{1,2,0:T(8,128)(2,1)S(1)}, u32[]{:S(2)}, u32[]{:S(2)}) %all-to-all-start) | async-done | bytes 131104 | tf_op jit(solution)/shard_map/all_to_all | solution.py:106
  84.4 3.5 %all-to-all-start.1 = ((bf16[32,128,128]{2,1,0:T(8,128)(2,1)}), bf16[32,128,128]{2,1,0:T(8,128)(2,1)S(1)}, u32[]{:S(2)}, u32[]{:S(2)}) async-start(bf16[32,128,128]{2,1,0:T(8,128)(2,1)} %select_select_fusion), calls=%async_computation.1 | async-start | bytes 2097152 | tf_op jit(solution)/shard_map/all_to_all | solution.py:105
  88.0 10.9 %all-to-all-done.1 = bf16[32,128,128]{2,1,0:T(8,128)(2,1)S(1)} async-done(((bf16[32,128,128]{2,1,0:T(8,128)(2,1)}), bf16[32,128,128]{2,1,0:T(8,128)(2,1)S(1)}, u32[]{:S(2)}, u32[]{:S(2)}) %all-to-all-start.1) | async-done | bytes 1048608 | tf_op jit(solution)/shard_map/all_to_all | solution.py:105
  98.9 78.2 %while.16 = (s32[]{:T(128)}, f32[1024,1024]{1,0:T(8,128)}, f32[8,128]{1,0:T(8,128)S(1)}, bf16[4096,16]{0,1:T(8,128)(2,1)S(1)}, bf16[4096,128]{1,0:T(8,128)(2,1)S...) while((s32[]{:T(128)}, f32[1024,1024]{1,0:T(8,128)}, f32[8,128]{1,0:T(8,128)S(1)}, ...), condition=%wide.region_7.8_spmd.clone, body=%wide.region_6.7_spmd.clone.sunk | while | flops 1216682112 | bytes 66151160 | solution.py:70
  100.2 1.6 fusion.34
  102.2 1.8 copy-done.1
  103.9 2.7 %fusion.36 = f32[1024,1024]{1,0:T(8,128)S(1)} fusion(f32[128,8,8,128]{3,2,1,0:T(8,128)S(1)} %bitcast.61, f32[1024,1152]{1,0:T(8,128)S(1)} %fusion.34, f32[1024,1024]{1,0:T(8,128)S(1)} %copy-done.1, pred[]{:T(512)S(6)} %compare.8), kind=kLoop, calls=%fused_computation.3.clone.1 | loop fusion | flops 3145728 | bytes 16777216 | tf_op jit(solution)/shard_map/while/body/eval_jaxpr/sub | solution.py:66
  106.6 2.0 %copy-done.2 = f32[1024,1024]{1,0:T(8,128)} copy-done((f32[1024,1024]{1,0:T(8,128)}, f32[1024,1024]{1,0:T(8,128)S(1)}, u32[]{:S(2)}) %copy-start.2) | copy-done | bytes 4194328 | tf_op jit(solution)/shard_map/while
  109.9 1.6 fusion.34
  111.9 1.8 copy-done.1
  113.7 2.7 %fusion.36 = f32[1024,1024]{1,0:T(8,128)S(1)} fusion(f32[128,8,8,128]{3,2,1,0:T(8,128)S(1)} %bitcast.61, f32[1024,1152]{1,0:T(8,128)S(1)} %fusion.34, f32[1024,1024]{1,0:T(8,128)S(1)} %copy-done.1, pred[]{:T(512)S(6)} %compare.8), kind=kLoop, calls=%fused_computation.3.clone.1 | loop fusion | flops 3145728 | bytes 16777216 | tf_op jit(solution)/shard_map/while/body/eval_jaxpr/sub | solution.py:66
  116.4 2.0 %copy-done.2 = f32[1024,1024]{1,0:T(8,128)} copy-done((f32[1024,1024]{1,0:T(8,128)}, f32[1024,1024]{1,0:T(8,128)S(1)}, u32[]{:S(2)}) %copy-start.2) | copy-done | bytes 4194328 | tf_op jit(solution)/shard_map/while
  119.7 1.6 fusion.34
  121.7 1.8 copy-done.1
  123.5 2.7 %fusion.36 = f32[1024,1024]{1,0:T(8,128)S(1)} fusion(f32[128,8,8,128]{3,2,1,0:T(8,128)S(1)} %bitcast.61, f32[1024,1152]{1,0:T(8,128)S(1)} %fusion.34, f32[1024,1024]{1,0:T(8,128)S(1)} %copy-done.1, pred[]{:T(512)S(6)} %compare.8), kind=kLoop, calls=%fused_computation.3.clone.1 | loop fusion | flops 3145728 | bytes 16777216 | tf_op jit(solution)/shard_map/while/body/eval_jaxpr/sub | solution.py:66
  126.2 2.0 %copy-done.2 = f32[1024,1024]{1,0:T(8,128)} copy-done((f32[1024,1024]{1,0:T(8,128)}, f32[1024,1024]{1,0:T(8,128)S(1)}, u32[]{:S(2)}) %copy-start.2) | copy-done | bytes 4194328 | tf_op jit(solution)/shard_map/while
  129.5 1.6 fusion.34
  131.5 1.8 copy-done.1
  133.3 2.7 %fusion.36 = f32[1024,1024]{1,0:T(8,128)S(1)} fusion(f32[128,8,8,128]{3,2,1,0:T(8,128)S(1)} %bitcast.61, f32[1024,1152]{1,0:T(8,128)S(1)} %fusion.34, f32[1024,1024]{1,0:T(8,128)S(1)} %copy-done.1, pred[]{:T(512)S(6)} %compare.8), kind=kLoop, calls=%fused_computation.3.clone.1 | loop fusion | flops 3145728 | bytes 16777216 | tf_op jit(solution)/shard_map/while/body/eval_jaxpr/sub | solution.py:66
  136.0 2.0 %copy-done.2 = f32[1024,1024]{1,0:T(8,128)} copy-done((f32[1024,1024]{1,0:T(8,128)}, f32[1024,1024]{1,0:T(8,128)S(1)}, u32[]{:S(2)}) %copy-start.2) | copy-done | bytes 4194328 | tf_op jit(solution)/shard_map/while
  139.3 1.6 fusion.34
  141.3 1.8 copy-done.1
  143.1 2.7 %fusion.36 = f32[1024,1024]{1,0:T(8,128)S(1)} fusion(f32[128,8,8,128]{3,2,1,0:T(8,128)S(1)} %bitcast.61, f32[1024,1152]{1,0:T(8,128)S(1)} %fusion.34, f32[1024,1024]{1,0:T(8,128)S(1)} %copy-done.1, pred[]{:T(512)S(6)} %compare.8), kind=kLoop, calls=%fused_computation.3.clone.1 | loop fusion | flops 3145728 | bytes 16777216 | tf_op jit(solution)/shard_map/while/body/eval_jaxpr/sub | solution.py:66
  145.8 2.0 %copy-done.2 = f32[1024,1024]{1,0:T(8,128)} copy-done((f32[1024,1024]{1,0:T(8,128)}, f32[1024,1024]{1,0:T(8,128)S(1)}, u32[]{:S(2)}) %copy-start.2) | copy-done | bytes 4194328 | tf_op jit(solution)/shard_map/while
  149.1 1.6 fusion.34
  151.1 1.8 copy-done.1
  152.8 2.7 %fusion.36 = f32[1024,1024]{1,0:T(8,128)S(1)} fusion(f32[128,8,8,128]{3,2,1,0:T(8,128)S(1)} %bitcast.61, f32[1024,1152]{1,0:T(8,128)S(1)} %fusion.34, f32[1024,1024]{1,0:T(8,128)S(1)} %copy-done.1, pred[]{:T(512)S(6)} %compare.8), kind=kLoop, calls=%fused_computation.3.clone.1 | loop fusion | flops 3145728 | bytes 16777216 | tf_op jit(solution)/shard_map/while/body/eval_jaxpr/sub | solution.py:66
  155.5 2.0 %copy-done.2 = f32[1024,1024]{1,0:T(8,128)} copy-done((f32[1024,1024]{1,0:T(8,128)}, f32[1024,1024]{1,0:T(8,128)S(1)}, u32[]{:S(2)}) %copy-start.2) | copy-done | bytes 4194328 | tf_op jit(solution)/shard_map/while
  158.8 1.6 fusion.34
  160.9 1.8 copy-done.1
  162.6 2.7 %fusion.36 = f32[1024,1024]{1,0:T(8,128)S(1)} fusion(f32[128,8,8,128]{3,2,1,0:T(8,128)S(1)} %bitcast.61, f32[1024,1152]{1,0:T(8,128)S(1)} %fusion.34, f32[1024,1024]{1,0:T(8,128)S(1)} %copy-done.1, pred[]{:T(512)S(6)} %compare.8), kind=kLoop, calls=%fused_computation.3.clone.1 | loop fusion | flops 3145728 | bytes 16777216 | tf_op jit(solution)/shard_map/while/body/eval_jaxpr/sub | solution.py:66
  165.3 2.0 %copy-done.2 = f32[1024,1024]{1,0:T(8,128)} copy-done((f32[1024,1024]{1,0:T(8,128)}, f32[1024,1024]{1,0:T(8,128)S(1)}, u32[]{:S(2)}) %copy-start.2) | copy-done | bytes 4194328 | tf_op jit(solution)/shard_map/while
  168.6 1.6 fusion.34
  170.6 1.8 copy-done.1
  172.4 2.7 %fusion.36 = f32[1024,1024]{1,0:T(8,128)S(1)} fusion(f32[128,8,8,128]{3,2,1,0:T(8,128)S(1)} %bitcast.61, f32[1024,1152]{1,0:T(8,128)S(1)} %fusion.34, f32[1024,1024]{1,0:T(8,128)S(1)} %copy-done.1, pred[]{:T(512)S(6)} %compare.8), kind=kLoop, calls=%fused_computation.3.clone.1 | loop fusion | flops 3145728 | bytes 16777216 | tf_op jit(solution)/shard_map/while/body/eval_jaxpr/sub | solution.py:66
  175.1 2.0 %copy-done.2 = f32[1024,1024]{1,0:T(8,128)} copy-done((f32[1024,1024]{1,0:T(8,128)}, f32[1024,1024]{1,0:T(8,128)S(1)}, u32[]{:S(2)}) %copy-start.2) | copy-done | bytes 4194328 | tf_op jit(solution)/shard_map/while
  177.7 5.0 %multiply_bitcast_fusion = f32[1,1024,1024]{2,1,0:T(8,128)} fusion(f32[1024,1024]{1,0:T(8,128)} %get-tuple-element.97), kind=kLoop, calls=%fused_computation.18 | loop fusion | flops 1048576 | bytes 8388608 | tf_op jit(solution)/shard_map/broadcast_in_dim | solution.py:111
  (105 shorter events, 16.1 us)
Async XLA Ops:
  7.2 10.5 %copy-start = (bf16[2048,128]{1,0:T(8,128)(2,1)S(1)}, bf16[2048,128]{1,0:T(8,128)(2,1)}, u32[]{:S(2)}) copy-start(bf16[2048,128]{1,0:T(8,128)(2,1)} %param.6) | copy-start | bytes 1572868
  7.2 65.4 %all-reduce.2.cloned.1.call-start = ((), (), s32[]{:S(2)}) async-start(), calls=%async_computation.2 | async-start | bytes 131072 | tf_op jit(solution)/shard_map/psum | solution.py:89
  75.8 8.7 %all-to-all-start = ((bf16[32,128,16]{1,2,0:T(8,128)(2,1)}), bf16[32,128,16]{1,2,0:T(8,128)(2,1)S(1)}, u32[]{:S(2)}, u32[]{:S(2)}) async-start(bf16[32,128,16]{1,2,0:T(8,128)(2,1)} %select_select_fusion.1), calls=%async_computation | async-start | bytes 262144 | tf_op jit(solution)/shard_map/all_to_all | solution.py:106
  84.4 14.4 %all-to-all-start.1 = ((bf16[32,128,128]{2,1,0:T(8,128)(2,1)}), bf16[32,128,128]{2,1,0:T(8,128)(2,1)S(1)}, u32[]{:S(2)}, u32[]{:S(2)}) async-start(bf16[32,128,128]{2,1,0:T(8,128)(2,1)} %select_select_fusion), calls=%async_computation.1 | async-start | bytes 2097152 | tf_op jit(solution)/shard_map/all_to_all | solution.py:105
  101.7 2.2 %copy-start.1 = (f32[1024,1024]{1,0:T(8,128)S(1)}, f32[1024,1024]{1,0:T(8,128)}, u32[]{:S(2)}) copy-start(f32[1024,1024]{1,0:T(8,128)} %get-tuple-element.179) | copy-start | bytes 12582916 | tf_op jit(solution)/shard_map/while
  106.6 2.0 %copy-start.2 = (f32[1024,1024]{1,0:T(8,128)}, f32[1024,1024]{1,0:T(8,128)S(1)}, u32[]{:S(2)}) copy-start(f32[1024,1024]{1,0:T(8,128)S(1)} %fusion.36) | copy-start | bytes 12582916 | tf_op jit(solution)/shard_map/while
  111.5 2.2 %copy-start.1 = (f32[1024,1024]{1,0:T(8,128)S(1)}, f32[1024,1024]{1,0:T(8,128)}, u32[]{:S(2)}) copy-start(f32[1024,1024]{1,0:T(8,128)} %get-tuple-element.179) | copy-start | bytes 12582916 | tf_op jit(solution)/shard_map/while
  116.4 2.0 %copy-start.2 = (f32[1024,1024]{1,0:T(8,128)}, f32[1024,1024]{1,0:T(8,128)S(1)}, u32[]{:S(2)}) copy-start(f32[1024,1024]{1,0:T(8,128)S(1)} %fusion.36) | copy-start | bytes 12582916 | tf_op jit(solution)/shard_map/while
  121.3 2.2 %copy-start.1 = (f32[1024,1024]{1,0:T(8,128)S(1)}, f32[1024,1024]{1,0:T(8,128)}, u32[]{:S(2)}) copy-start(f32[1024,1024]{1,0:T(8,128)} %get-tuple-element.179) | copy-start | bytes 12582916 | tf_op jit(solution)/shard_map/while
  126.2 2.0 %copy-start.2 = (f32[1024,1024]{1,0:T(8,128)}, f32[1024,1024]{1,0:T(8,128)S(1)}, u32[]{:S(2)}) copy-start(f32[1024,1024]{1,0:T(8,128)S(1)} %fusion.36) | copy-start | bytes 12582916 | tf_op jit(solution)/shard_map/while
  131.1 2.2 %copy-start.1 = (f32[1024,1024]{1,0:T(8,128)S(1)}, f32[1024,1024]{1,0:T(8,128)}, u32[]{:S(2)}) copy-start(f32[1024,1024]{1,0:T(8,128)} %get-tuple-element.179) | copy-start | bytes 12582916 | tf_op jit(solution)/shard_map/while
  136.0 2.0 %copy-start.2 = (f32[1024,1024]{1,0:T(8,128)}, f32[1024,1024]{1,0:T(8,128)S(1)}, u32[]{:S(2)}) copy-start(f32[1024,1024]{1,0:T(8,128)S(1)} %fusion.36) | copy-start | bytes 12582916 | tf_op jit(solution)/shard_map/while
  140.9 2.2 %copy-start.1 = (f32[1024,1024]{1,0:T(8,128)S(1)}, f32[1024,1024]{1,0:T(8,128)}, u32[]{:S(2)}) copy-start(f32[1024,1024]{1,0:T(8,128)} %get-tuple-element.179) | copy-start | bytes 12582916 | tf_op jit(solution)/shard_map/while
  145.8 2.0 %copy-start.2 = (f32[1024,1024]{1,0:T(8,128)}, f32[1024,1024]{1,0:T(8,128)S(1)}, u32[]{:S(2)}) copy-start(f32[1024,1024]{1,0:T(8,128)S(1)} %fusion.36) | copy-start | bytes 12582916 | tf_op jit(solution)/shard_map/while
  150.6 2.2 %copy-start.1 = (f32[1024,1024]{1,0:T(8,128)S(1)}, f32[1024,1024]{1,0:T(8,128)}, u32[]{:S(2)}) copy-start(f32[1024,1024]{1,0:T(8,128)} %get-tuple-element.179) | copy-start | bytes 12582916 | tf_op jit(solution)/shard_map/while
  155.5 2.0 %copy-start.2 = (f32[1024,1024]{1,0:T(8,128)}, f32[1024,1024]{1,0:T(8,128)S(1)}, u32[]{:S(2)}) copy-start(f32[1024,1024]{1,0:T(8,128)S(1)} %fusion.36) | copy-start | bytes 12582916 | tf_op jit(solution)/shard_map/while
  160.4 2.2 %copy-start.1 = (f32[1024,1024]{1,0:T(8,128)S(1)}, f32[1024,1024]{1,0:T(8,128)}, u32[]{:S(2)}) copy-start(f32[1024,1024]{1,0:T(8,128)} %get-tuple-element.179) | copy-start | bytes 12582916 | tf_op jit(solution)/shard_map/while
  165.3 2.0 %copy-start.2 = (f32[1024,1024]{1,0:T(8,128)}, f32[1024,1024]{1,0:T(8,128)S(1)}, u32[]{:S(2)}) copy-start(f32[1024,1024]{1,0:T(8,128)S(1)} %fusion.36) | copy-start | bytes 12582916 | tf_op jit(solution)/shard_map/while
  170.2 2.2 %copy-start.1 = (f32[1024,1024]{1,0:T(8,128)S(1)}, f32[1024,1024]{1,0:T(8,128)}, u32[]{:S(2)}) copy-start(f32[1024,1024]{1,0:T(8,128)} %get-tuple-element.179) | copy-start | bytes 12582916 | tf_op jit(solution)/shard_map/while
  175.1 2.0 %copy-start.2 = (f32[1024,1024]{1,0:T(8,128)}, f32[1024,1024]{1,0:T(8,128)S(1)}, u32[]{:S(2)}) copy-start(f32[1024,1024]{1,0:T(8,128)S(1)} %fusion.36) | copy-start | bytes 12582916 | tf_op jit(solution)/shard_map/while
Sparse Core Ops, SparseCore 0:
  18.7 53.8 all-reduce.1
where the time goes:
time: 190 us
  waiting for transfers between devices  65.6 us (35%)
  other arithmetic  42.1 us (22%)
  local copies, waits for them, and re-layouts  35.8 us (19%)
  matrix products  14.6 us (8%)
  between operations  14.1 us (7%)
  blocking collectives  9.63 us (5%)
  starting transfers between devices  7.2 us (4%)
    psum x1, waiting for transfers between devices, per_device(): logits = lax.psum(partial_logits, 'feat')  50.8 us
    while x40, local copies, waits for them, and re-layouts  32.4 us
    sub x8, other arithmetic, turn(): hess_acc + spread_diagonal(diag_part, classes, width) - square  21.6 us
    dot_general x8, matrix products, turn(): lax.dot_general(kron_rows, joint, (((0,), (0,)), ((), ())), preferred_ele...  12.6 us
    all_to_all x1, waiting for transfers between devices, per_device(): lax.all_to_all(sent_features, 'dp', split_axis=0, concat_axis=0, tiled=True)  10.9 us
    all_gather x1, blocking collectives, per_device(): gathered = lax.all_gather(weights, 'dp', axis=1, tiled=True)  9.63 us
    convert_element_type x8, other arithmetic, turn(): kron_rows = (probs[:, :, None] * x_part.astype(jnp.float32)[:, None, :])....  5.53 us
    broadcast_in_dim x1, other arithmetic, per_device(): hessian = (hess_acc / block_rows)[None]  5.04 us
  transfers between devices with their start and end apart: 3, of which 3 were waited for; matrix products, arithmetic and copies ran while one was open for 2% of the time, Pallas kernels for 0%

commit v1 on v0

--- a/solution.py
+++ b/solution.py
@@ -86,7 +86,7 @@
         jnp.float32
     )
     partial_logits = jnp.sum(every_owner * owner_mask[:, :, None], axis=1)
-    logits = lax.psum(partial_logits, "feat")
+    logits = jnp.sum(lax.all_gather(partial_logits, "feat"), axis=0)
     probs = normalize(logits)
     onehot = (labels[:, None] == jnp.arange(classes, dtype=jnp.int32)[None, :]).astype(jnp.float32)
     probs_half = probs.astype(jnp.bfloat16)

time: 190 us -> 141 us (0.74)
  waiting for transfers between devices: 65.6 us -> 16.3 us
  blocking collectives: 9.63 us -> 25 us
  between operations: 14.1 us -> 0.73 us
    psum x1 -> x0, waiting for transfers between devices: 50.8 us -> none  [per_device(): logits = lax.psum(partial_logits, 'feat')]
    all_gather x0 -> x1, blocking collectives: none -> 15.4 us  [per_device(): logits = jnp.sum(lax.all_gather(partial_logits, 'feat'), axis=0)]
    all_to_all x1, waiting for transfers between devices: 10.9 us -> 13.2 us  [per_device(): lax.all_to_all(sent_features, 'dp', split_axis=0, concat_axis=0, tiled=True)]
  transfers between devices with their start and end apart: 3 -> 2, of which waited for: 3 -> 2; matrix products, arithmetic and copies ran while one was open for 2% -> 1% of each run, Pallas kernels for 0% -> 0%
where the time goes in v1:
time: 141 us; the launch traced here: 140 us
  other arithmetic  41.2 us (29%)
  local copies, waits for them, and re-layouts  35.8 us (25%)
  blocking collectives  25 us (18%)
  waiting for transfers between devices  16.3 us (12%)
  matrix products  13.9 us (10%)
  starting transfers between devices  6.84 us (5%)
    while x40, local copies, waits for them, and re-layouts  32.4 us
    sub x8, other arithmetic, turn(): hess_acc + spread_diagonal(diag_part, classes, width) - square  21.6 us
    all_gather x1, blocking collectives, per_device(): logits = jnp.sum(lax.all_gather(partial_logits, 'feat'), axis=0)  15.4 us
    all_to_all x1, waiting for transfers between devices, per_device(): lax.all_to_all(sent_features, 'dp', split_axis=0, concat_axis=0, tiled=True)  13.2 us
    dot_general x8, matrix products, turn(): lax.dot_general(kron_rows, joint, (((0,), (0,)), ((), ())), preferred_ele...  12.6 us
    all_gather x1, blocking collectives, per_device(): gathered = lax.all_gather(weights, 'dp', axis=1, tiled=True)  9.63 us
    convert_element_type x8, other arithmetic, turn(): kron_rows = (probs[:, :, None] * x_part.astype(jnp.float32)[:, None, :])....  5.53 us
    broadcast_in_dim x1, other arithmetic, per_device(): hessian = (hess_acc / block_rows)[None]  5.04 us
  transfers between devices with their start and end apart: 2, of which 2 were waited for; matrix products, arithmetic and copies ran while one was open for 1% of the time, Pallas kernels for 0%

profile of v1, /device:TPU:0, one launch (start us, length us, event | category | flops | bytes accessed | tf_op | source)
XLA Modules:
  0.0 140.4 jit_solution(6626834343008648804)
XLA Ops:
  0.7 0.9 convert_reduce_fusion
  1.6 0.7 select_reduce_fusion
  2.3 0.7 fusion.15
  3.1 0.7 broadcast_bitcast_fusion
  3.8 9.6 %all_gather.9 = bf16[8,512]{1,0:T(8,128)(2,1)S(1)} all-gather(bf16[8,128]{1,0:T(8,128)(2,1)} %param.8), channel_id=1, replica_groups=mesh['dp'=4,'feat'=8] {'dp'}, dimensions={1}, use_global_device_ids=true | all-gather | bytes 10240 | tf_op jit(solution)/shard_map/all_gather | solution.py:81
  13.7 15.4 %all-gather = f32[16384,8]{0,1:T(8,128)S(1)} all-gather(f32[2048,8]{0,1:T(8,128)S(1)} %fusion.9), channel_id=2, replica_groups=mesh['dp'=4,'feat'=8] {'feat'}, dimensions={0}, use_global_device_ids=true | all-gather | bytes 589824 | tf_op jit(solution)/shard_map/all_gather | solution.py:89
  29.2 0.7 fusion.11
  30.6 0.8 select_select_fusion.1
  31.4 3.3 %all-to-all-start = ((bf16[32,128,16]{1,2,0:T(8,128)(2,1)}), bf16[32,128,16]{1,2,0:T(8,128)(2,1)S(1)}, u32[]{:S(2)}, u32[]{:S(2)}) async-start(bf16[32,128,16]{1,2,0:T(8,128)(2,1)} %select_select_fusion.1), calls=%async_computation | async-start | bytes 262144 | tf_op jit(solution)/shard_map/all_to_all | solution.py:106
  34.7 0.7 gather_fusion.1
  35.4 1.2 select_select_fusion
  36.6 3.1 %all-to-all-done = bf16[32,128,16]{1,2,0:T(8,128)(2,1)S(1)} async-done(((bf16[32,128,16]{1,2,0:T(8,128)(2,1)}), bf16[32,128,16]{1,2,0:T(8,128)(2,1)S(1)}, u32[]{:S(2)}, u32[]{:S(2)}) %all-to-all-start) | async-done | bytes 131104 | tf_op jit(solution)/shard_map/all_to_all | solution.py:106
  39.8 3.5 %all-to-all-start.1 = ((bf16[32,128,128]{2,1,0:T(8,128)(2,1)}), bf16[32,128,128]{2,1,0:T(8,128)(2,1)S(1)}, u32[]{:S(2)}, u32[]{:S(2)}) async-start(bf16[32,128,128]{2,1,0:T(8,128)(2,1)} %select_select_fusion), calls=%async_computation.1 | async-start | bytes 2097152 | tf_op jit(solution)/shard_map/all_to_all | solution.py:105
  43.3 13.2 %all-to-all-done.1 = bf16[32,128,128]{2,1,0:T(8,128)(2,1)S(1)} async-done(((bf16[32,128,128]{2,1,0:T(8,128)(2,1)}), bf16[32,128,128]{2,1,0:T(8,128)(2,1)S(1)}, u32[]{:S(2)}, u32[]{:S(2)}) %all-to-all-start.1) | async-done | bytes 1048608 | tf_op jit(solution)/shard_map/all_to_all | solution.py:105
  56.5 78.2 %while.16 = (s32[]{:T(128)}, f32[1024,1024]{1,0:T(8,128)}, f32[8,128]{1,0:T(8,128)S(1)}, bf16[4096,16]{0,1:T(8,128)(2,1)S(1)}, bf16[4096,128]{1,0:T(8,128)(2,1)S...) while((s32[]{:T(128)}, f32[1024,1024]{1,0:T(8,128)}, f32[8,128]{1,0:T(8,128)S(1)}, ...), condition=%wide.region_7.8_spmd.clone, body=%wide.region_6.7_spmd.clone.sunk | while | flops 1216682112 | bytes 66151160 | solution.py:70
  57.8 1.6 %fusion.34 = f32[1024,1152]{1,0:T(8,128)S(1)} fusion(bf16[512,1024]{1,0:T(8,128)(2,1)S(1)} %bitcast.68, bf16[512,128]{1,0:T(8,128)(2,1)S(1)} %get-tuple-element.167), kind=kOutput, calls=%fused_computation.6.clone.1 | convolution fusion | flops 1210318848 | bytes 5898240 | tf_op jit(solution)/shard_map/while/body/eval_jaxpr/dot_general | solution.py:57
  59.8 1.8 %copy-done.1 = f32[1024,1024]{1,0:T(8,128)S(1)} copy-done((f32[1024,1024]{1,0:T(8,128)S(1)}, f32[1024,1024]{1,0:T(8,128)}, u32[]{:S(2)}) %copy-start.1) | copy-done | bytes 4194328 | tf_op jit(solution)/shard_map/while
  61.6 2.7 %fusion.36 = f32[1024,1024]{1,0:T(8,128)S(1)} fusion(f32[128,8,8,128]{3,2,1,0:T(8,128)S(1)} %bitcast.65, f32[1024,1152]{1,0:T(8,128)S(1)} %fusion.34, f32[1024,1024]{1,0:T(8,128)S(1)} %copy-done.1, pred[]{:T(512)S(6)} %compare.8), kind=kLoop, calls=%fused_computation.3.clone.1 | loop fusion | flops 3145728 | bytes 16777216 | tf_op jit(solution)/shard_map/while/body/eval_jaxpr/sub | solution.py:66
  64.3 2.0 %copy-done.2 = f32[1024,1024]{1,0:T(8,128)} copy-done((f32[1024,1024]{1,0:T(8,128)}, f32[1024,1024]{1,0:T(8,128)S(1)}, u32[]{:S(2)}) %copy-start.2) | copy-done | bytes 4194328 | tf_op jit(solution)/shard_map/while
  67.6 1.6 %fusion.34 = f32[1024,1152]{1,0:T(8,128)S(1)} fusion(bf16[512,1024]{1,0:T(8,128)(2,1)S(1)} %bitcast.68, bf16[512,128]{1,0:T(8,128)(2,1)S(1)} %get-tuple-element.167), kind=kOutput, calls=%fused_computation.6.clone.1 | convolution fusion | flops 1210318848 | bytes 5898240 | tf_op jit(solution)/shard_map/while/body/eval_jaxpr/dot_general | solution.py:57
  69.6 1.8 %copy-done.1 = f32[1024,1024]{1,0:T(8,128)S(1)} copy-done((f32[1024,1024]{1,0:T(8,128)S(1)}, f32[1024,1024]{1,0:T(8,128)}, u32[]{:S(2)}) %copy-start.1) | copy-done | bytes 4194328 | tf_op jit(solution)/shard_map/while
  71.4 2.7 %fusion.36 = f32[1024,1024]{1,0:T(8,128)S(1)} fusion(f32[128,8,8,128]{3,2,1,0:T(8,128)S(1)} %bitcast.65, f32[1024,1152]{1,0:T(8,128)S(1)} %fusion.34, f32[1024,1024]{1,0:T(8,128)S(1)} %copy-done.1, pred[]{:T(512)S(6)} %compare.8), kind=kLoop, calls=%fused_computation.3.clone.1 | loop fusion | flops 3145728 | bytes 16777216 | tf_op jit(solution)/shard_map/while/body/eval_jaxpr/sub | solution.py:66
  74.1 2.0 %copy-done.2 = f32[1024,1024]{1,0:T(8,128)} copy-done((f32[1024,1024]{1,0:T(8,128)}, f32[1024,1024]{1,0:T(8,128)S(1)}, u32[]{:S(2)}) %copy-start.2) | copy-done | bytes 4194328 | tf_op jit(solution)/shard_map/while
  77.4 1.6 %fusion.34 = f32[1024,1152]{1,0:T(8,128)S(1)} fusion(bf16[512,1024]{1,0:T(8,128)(2,1)S(1)} %bitcast.68, bf16[512,128]{1,0:T(8,128)(2,1)S(1)} %get-tuple-element.167), kind=kOutput, calls=%fused_computation.6.clone.1 | convolution fusion | flops 1210318848 | bytes 5898240 | tf_op jit(solution)/shard_map/while/body/eval_jaxpr/dot_general | solution.py:57
  79.4 1.8 %copy-done.1 = f32[1024,1024]{1,0:T(8,128)S(1)} copy-done((f32[1024,1024]{1,0:T(8,128)S(1)}, f32[1024,1024]{1,0:T(8,128)}, u32[]{:S(2)}) %copy-start.1) | copy-done | bytes 4194328 | tf_op jit(solution)/shard_map/while
  81.1 2.7 %fusion.36 = f32[1024,1024]{1,0:T(8,128)S(1)} fusion(f32[128,8,8,128]{3,2,1,0:T(8,128)S(1)} %bitcast.65, f32[1024,1152]{1,0:T(8,128)S(1)} %fusion.34, f32[1024,1024]{1,0:T(8,128)S(1)} %copy-done.1, pred[]{:T(512)S(6)} %compare.8), kind=kLoop, calls=%fused_computation.3.clone.1 | loop fusion | flops 3145728 | bytes 16777216 | tf_op jit(solution)/shard_map/while/body/eval_jaxpr/sub | solution.py:66
  83.9 2.0 %copy-done.2 = f32[1024,1024]{1,0:T(8,128)} copy-done((f32[1024,1024]{1,0:T(8,128)}, f32[1024,1024]{1,0:T(8,128)S(1)}, u32[]{:S(2)}) %copy-start.2) | copy-done | bytes 4194328 | tf_op jit(solution)/shard_map/while
  87.2 1.6 %fusion.34 = f32[1024,1152]{1,0:T(8,128)S(1)} fusion(bf16[512,1024]{1,0:T(8,128)(2,1)S(1)} %bitcast.68, bf16[512,128]{1,0:T(8,128)(2,1)S(1)} %get-tuple-element.167), kind=kOutput, calls=%fused_computation.6.clone.1 | convolution fusion | flops 1210318848 | bytes 5898240 | tf_op jit(solution)/shard_map/while/body/eval_jaxpr/dot_general | solution.py:57
  89.2 1.8 %copy-done.1 = f32[1024,1024]{1,0:T(8,128)S(1)} copy-done((f32[1024,1024]{1,0:T(8,128)S(1)}, f32[1024,1024]{1,0:T(8,128)}, u32[]{:S(2)}) %copy-start.1) | copy-done | bytes 4194328 | tf_op jit(solution)/shard_map/while
  90.9 2.7 %fusion.36 = f32[1024,1024]{1,0:T(8,128)S(1)} fusion(f32[128,8,8,128]{3,2,1,0:T(8,128)S(1)} %bitcast.65, f32[1024,1152]{1,0:T(8,128)S(1)} %fusion.34, f32[1024,1024]{1,0:T(8,128)S(1)} %copy-done.1, pred[]{:T(512)S(6)} %compare.8), kind=kLoop, calls=%fused_computation.3.clone.1 | loop fusion | flops 3145728 | bytes 16777216 | tf_op jit(solution)/shard_map/while/body/eval_jaxpr/sub | solution.py:66
  93.6 2.0 %copy-done.2 = f32[1024,1024]{1,0:T(8,128)} copy-done((f32[1024,1024]{1,0:T(8,128)}, f32[1024,1024]{1,0:T(8,128)S(1)}, u32[]{:S(2)}) %copy-start.2) | copy-done | bytes 4194328 | tf_op jit(solution)/shard_map/while
  96.9 1.6 %fusion.34 = f32[1024,1152]{1,0:T(8,128)S(1)} fusion(bf16[512,1024]{1,0:T(8,128)(2,1)S(1)} %bitcast.68, bf16[512,128]{1,0:T(8,128)(2,1)S(1)} %get-tuple-element.167), kind=kOutput, calls=%fused_computation.6.clone.1 | convolution fusion | flops 1210318848 | bytes 5898240 | tf_op jit(solution)/shard_map/while/body/eval_jaxpr/dot_general | solution.py:57
  98.9 1.8 %copy-done.1 = f32[1024,1024]{1,0:T(8,128)S(1)} copy-done((f32[1024,1024]{1,0:T(8,128)S(1)}, f32[1024,1024]{1,0:T(8,128)}, u32[]{:S(2)}) %copy-start.1) | copy-done | bytes 4194328 | tf_op jit(solution)/shard_map/while
  100.7 2.7 %fusion.36 = f32[1024,1024]{1,0:T(8,128)S(1)} fusion(f32[128,8,8,128]{3,2,1,0:T(8,128)S(1)} %bitcast.65, f32[1024,1152]{1,0:T(8,128)S(1)} %fusion.34, f32[1024,1024]{1,0:T(8,128)S(1)} %copy-done.1, pred[]{:T(512)S(6)} %compare.8), kind=kLoop, calls=%fused_computation.3.clone.1 | loop fusion | flops 3145728 | bytes 16777216 | tf_op jit(solution)/shard_map/while/body/eval_jaxpr/sub | solution.py:66
  103.4 2.0 %copy-done.2 = f32[1024,1024]{1,0:T(8,128)} copy-done((f32[1024,1024]{1,0:T(8,128)}, f32[1024,1024]{1,0:T(8,128)S(1)}, u32[]{:S(2)}) %copy-start.2) | copy-done | bytes 4194328 | tf_op jit(solution)/shard_map/while
  106.7 1.6 %fusion.34 = f32[1024,1152]{1,0:T(8,128)S(1)} fusion(bf16[512,1024]{1,0:T(8,128)(2,1)S(1)} %bitcast.68, bf16[512,128]{1,0:T(8,128)(2,1)S(1)} %get-tuple-element.167), kind=kOutput, calls=%fused_computation.6.clone.1 | convolution fusion | flops 1210318848 | bytes 5898240 | tf_op jit(solution)/shard_map/while/body/eval_jaxpr/dot_general | solution.py:57
  108.7 1.8 %copy-done.1 = f32[1024,1024]{1,0:T(8,128)S(1)} copy-done((f32[1024,1024]{1,0:T(8,128)S(1)}, f32[1024,1024]{1,0:T(8,128)}, u32[]{:S(2)}) %copy-start.1) | copy-done | bytes 4194328 | tf_op jit(solution)/shard_map/while
  110.5 2.7 %fusion.36 = f32[1024,1024]{1,0:T(8,128)S(1)} fusion(f32[128,8,8,128]{3,2,1,0:T(8,128)S(1)} %bitcast.65, f32[1024,1152]{1,0:T(8,128)S(1)} %fusion.34, f32[1024,1024]{1,0:T(8,128)S(1)} %copy-done.1, pred[]{:T(512)S(6)} %compare.8), kind=kLoop, calls=%fused_computation.3.clone.1 | loop fusion | flops 3145728 | bytes 16777216 | tf_op jit(solution)/shard_map/while/body/eval_jaxpr/sub | solution.py:66
  113.2 2.0 %copy-done.2 = f32[1024,1024]{1,0:T(8,128)} copy-done((f32[1024,1024]{1,0:T(8,128)}, f32[1024,1024]{1,0:T(8,128)S(1)}, u32[]{:S(2)}) %copy-start.2) | copy-done | bytes 4194328 | tf_op jit(solution)/shard_map/while
  116.5 1.6 %fusion.34 = f32[1024,1152]{1,0:T(8,128)S(1)} fusion(bf16[512,1024]{1,0:T(8,128)(2,1)S(1)} %bitcast.68, bf16[512,128]{1,0:T(8,128)(2,1)S(1)} %get-tuple-element.167), kind=kOutput, calls=%fused_computation.6.clone.1 | convolution fusion | flops 1210318848 | bytes 5898240 | tf_op jit(solution)/shard_map/while/body/eval_jaxpr/dot_general | solution.py:57
  118.5 1.8 %copy-done.1 = f32[1024,1024]{1,0:T(8,128)S(1)} copy-done((f32[1024,1024]{1,0:T(8,128)S(1)}, f32[1024,1024]{1,0:T(8,128)}, u32[]{:S(2)}) %copy-start.1) | copy-done | bytes 4194328 | tf_op jit(solution)/shard_map/while
  120.3 2.7 %fusion.36 = f32[1024,1024]{1,0:T(8,128)S(1)} fusion(f32[128,8,8,128]{3,2,1,0:T(8,128)S(1)} %bitcast.65, f32[1024,1152]{1,0:T(8,128)S(1)} %fusion.34, f32[1024,1024]{1,0:T(8,128)S(1)} %copy-done.1, pred[]{:T(512)S(6)} %compare.8), kind=kLoop, calls=%fused_computation.3.clone.1 | loop fusion | flops 3145728 | bytes 16777216 | tf_op jit(solution)/shard_map/while/body/eval_jaxpr/sub | solution.py:66
  123.0 2.0 %copy-done.2 = f32[1024,1024]{1,0:T(8,128)} copy-done((f32[1024,1024]{1,0:T(8,128)}, f32[1024,1024]{1,0:T(8,128)S(1)}, u32[]{:S(2)}) %copy-start.2) | copy-done | bytes 4194328 | tf_op jit(solution)/shard_map/while
  126.3 1.6 %fusion.34 = f32[1024,1152]{1,0:T(8,128)S(1)} fusion(bf16[512,1024]{1,0:T(8,128)(2,1)S(1)} %bitcast.68, bf16[512,128]{1,0:T(8,128)(2,1)S(1)} %get-tuple-element.167), kind=kOutput, calls=%fused_computation.6.clone.1 | convolution fusion | flops 1210318848 | bytes 5898240 | tf_op jit(solution)/shard_map/while/body/eval_jaxpr/dot_general | solution.py:57
  128.3 1.8 %copy-done.1 = f32[1024,1024]{1,0:T(8,128)S(1)} copy-done((f32[1024,1024]{1,0:T(8,128)S(1)}, f32[1024,1024]{1,0:T(8,128)}, u32[]{:S(2)}) %copy-start.1) | copy-done | bytes 4194328 | tf_op jit(solution)/shard_map/while
  130.0 2.7 %fusion.36 = f32[1024,1024]{1,0:T(8,128)S(1)} fusion(f32[128,8,8,128]{3,2,1,0:T(8,128)S(1)} %bitcast.65, f32[1024,1152]{1,0:T(8,128)S(1)} %fusion.34, f32[1024,1024]{1,0:T(8,128)S(1)} %copy-done.1, pred[]{:T(512)S(6)} %compare.8), kind=kLoop, calls=%fused_computation.3.clone.1 | loop fusion | flops 3145728 | bytes 16777216 | tf_op jit(solution)/shard_map/while/body/eval_jaxpr/sub | solution.py:66
  132.8 2.0 %copy-done.2 = f32[1024,1024]{1,0:T(8,128)} copy-done((f32[1024,1024]{1,0:T(8,128)}, f32[1024,1024]{1,0:T(8,128)S(1)}, u32[]{:S(2)}) %copy-start.2) | copy-done | bytes 4194328 | tf_op jit(solution)/shard_map/while
  135.4 5.0 %multiply_bitcast_fusion = f32[1,1024,1024]{2,1,0:T(8,128)} fusion(f32[1024,1024]{1,0:T(8,128)} %get-tuple-element.97), kind=kLoop, calls=%fused_computation.18 | loop fusion | flops 1048576 | bytes 8388608 | tf_op jit(solution)/shard_map/broadcast_in_dim | solution.py:111
  (104 shorter events, 14.9 us)
Async XLA Ops:
  0.6 12.8 %copy-start = (bf16[2048,128]{1,0:T(8,128)(2,1)S(1)}, bf16[2048,128]{1,0:T(8,128)(2,1)}, u32[]{:S(2)}) copy-start(bf16[2048,128]{1,0:T(8,128)(2,1)} %param.6) | copy-start | bytes 1572868
  31.4 8.4 %all-to-all-start = ((bf16[32,128,16]{1,2,0:T(8,128)(2,1)}), bf16[32,128,16]{1,2,0:T(8,128)(2,1)S(1)}, u32[]{:S(2)}, u32[]{:S(2)}) async-start(bf16[32,128,16]{1,2,0:T(8,128)(2,1)} %select_select_fusion.1), calls=%async_computation | async-start | bytes 262144 | tf_op jit(solution)/shard_map/all_to_all | solution.py:106
  39.8 16.8 %all-to-all-start.1 = ((bf16[32,128,128]{2,1,0:T(8,128)(2,1)}), bf16[32,128,128]{2,1,0:T(8,128)(2,1)S(1)}, u32[]{:S(2)}, u32[]{:S(2)}) async-start(bf16[32,128,128]{2,1,0:T(8,128)(2,1)} %select_select_fusion), calls=%async_computation.1 | async-start | bytes 2097152 | tf_op jit(solution)/shard_map/all_to_all | solution.py:105
  59.4 2.2 %copy-start.1 = (f32[1024,1024]{1,0:T(8,128)S(1)}, f32[1024,1024]{1,0:T(8,128)}, u32[]{:S(2)}) copy-start(f32[1024,1024]{1,0:T(8,128)} %get-tuple-element.179) | copy-start | bytes 12582916 | tf_op jit(solution)/shard_map/while
  64.3 2.0 %copy-start.2 = (f32[1024,1024]{1,0:T(8,128)}, f32[1024,1024]{1,0:T(8,128)S(1)}, u32[]{:S(2)}) copy-start(f32[1024,1024]{1,0:T(8,128)S(1)} %fusion.36) | copy-start | bytes 12582916 | tf_op jit(solution)/shard_map/while
  69.2 2.2 %copy-start.1 = (f32[1024,1024]{1,0:T(8,128)S(1)}, f32[1024,1024]{1,0:T(8,128)}, u32[]{:S(2)}) copy-start(f32[1024,1024]{1,0:T(8,128)} %get-tuple-element.179) | copy-start | bytes 12582916 | tf_op jit(solution)/shard_map/while
  74.1 2.0 %copy-start.2 = (f32[1024,1024]{1,0:T(8,128)}, f32[1024,1024]{1,0:T(8,128)S(1)}, u32[]{:S(2)}) copy-start(f32[1024,1024]{1,0:T(8,128)S(1)} %fusion.36) | copy-start | bytes 12582916 | tf_op jit(solution)/shard_map/while
  79.0 2.2 %copy-start.1 = (f32[1024,1024]{1,0:T(8,128)S(1)}, f32[1024,1024]{1,0:T(8,128)}, u32[]{:S(2)}) copy-start(f32[1024,1024]{1,0:T(8,128)} %get-tuple-element.179) | copy-start | bytes 12582916 | tf_op jit(solution)/shard_map/while
  83.8 2.0 %copy-start.2 = (f32[1024,1024]{1,0:T(8,128)}, f32[1024,1024]{1,0:T(8,128)S(1)}, u32[]{:S(2)}) copy-start(f32[1024,1024]{1,0:T(8,128)S(1)} %fusion.36) | copy-start | bytes 12582916 | tf_op jit(solution)/shard_map/while
  88.7 2.2 %copy-start.1 = (f32[1024,1024]{1,0:T(8,128)S(1)}, f32[1024,1024]{1,0:T(8,128)}, u32[]{:S(2)}) copy-start(f32[1024,1024]{1,0:T(8,128)} %get-tuple-element.179) | copy-start | bytes 12582916 | tf_op jit(solution)/shard_map/while
  93.6 2.0 %copy-start.2 = (f32[1024,1024]{1,0:T(8,128)}, f32[1024,1024]{1,0:T(8,128)S(1)}, u32[]{:S(2)}) copy-start(f32[1024,1024]{1,0:T(8,128)S(1)} %fusion.36) | copy-start | bytes 12582916 | tf_op jit(solution)/shard_map/while
  98.5 2.2 %copy-start.1 = (f32[1024,1024]{1,0:T(8,128)S(1)}, f32[1024,1024]{1,0:T(8,128)}, u32[]{:S(2)}) copy-start(f32[1024,1024]{1,0:T(8,128)} %get-tuple-element.179) | copy-start | bytes 12582916 | tf_op jit(solution)/shard_map/while
  103.4 2.0 %copy-start.2 = (f32[1024,1024]{1,0:T(8,128)}, f32[1024,1024]{1,0:T(8,128)S(1)}, u32[]{:S(2)}) copy-start(f32[1024,1024]{1,0:T(8,128)S(1)} %fusion.36) | copy-start | bytes 12582916 | tf_op jit(solution)/shard_map/while
  108.3 2.2 %copy-start.1 = (f32[1024,1024]{1,0:T(8,128)S(1)}, f32[1024,1024]{1,0:T(8,128)}, u32[]{:S(2)}) copy-start(f32[1024,1024]{1,0:T(8,128)} %get-tuple-element.179) | copy-start | bytes 12582916 | tf_op jit(solution)/shard_map/while
  113.2 2.0 %copy-start.2 = (f32[1024,1024]{1,0:T(8,128)}, f32[1024,1024]{1,0:T(8,128)S(1)}, u32[]{:S(2)}) copy-start(f32[1024,1024]{1,0:T(8,128)S(1)} %fusion.36) | copy-start | bytes 12582916 | tf_op jit(solution)/shard_map/while
  118.1 2.2 %copy-start.1 = (f32[1024,1024]{1,0:T(8,128)S(1)}, f32[1024,1024]{1,0:T(8,128)}, u32[]{:S(2)}) copy-start(f32[1024,1024]{1,0:T(8,128)} %get-tuple-element.179) | copy-start | bytes 12582916 | tf_op jit(solution)/shard_map/while
  123.0 2.0 %copy-start.2 = (f32[1024,1024]{1,0:T(8,128)}, f32[1024,1024]{1,0:T(8,128)S(1)}, u32[]{:S(2)}) copy-start(f32[1024,1024]{1,0:T(8,128)S(1)} %fusion.36) | copy-start | bytes 12582916 | tf_op jit(solution)/shard_map/while
  127.9 2.2 %copy-start.1 = (f32[1024,1024]{1,0:T(8,128)S(1)}, f32[1024,1024]{1,0:T(8,128)}, u32[]{:S(2)}) copy-start(f32[1024,1024]{1,0:T(8,128)} %get-tuple-element.179) | copy-start | bytes 12582916 | tf_op jit(solution)/shard_map/while
  132.7 2.0 %copy-start.2 = (f32[1024,1024]{1,0:T(8,128)}, f32[1024,1024]{1,0:T(8,128)S(1)}, u32[]{:S(2)}) copy-start(f32[1024,1024]{1,0:T(8,128)S(1)} %fusion.36) | copy-start | bytes 12582916 | tf_op jit(solution)/shard_map/while
